TPU v7x, 32 devices: a whole 2x2x4 slice. The times are simulated.
32 devices in a mesh: cand: 4 (over x, core), seq: 8 (over z, y).
Axes of the slice: x: 2, y: 2, z: 4, core: 2. Of those that a mesh axis runs over, the one named last changes fastest.
Arguments:
- latent: bfloat16 [4, 384, 3072], P('cand', 'seq'), may hold values from -0.59765625 to 0.59765625
- timesteps: int32 [4], replicated, may hold values from 0 to 999
- positions: int32 [3, 384], replicated, may hold values from 0 to 63
- mod_weight: bfloat16 [3072, 9216], P('cand', 'seq'), may hold values from -0.109375 to 0.109375
- input_weight: bfloat16 [3072, 16, 384], P('cand', 'seq'), may hold values from -0.109375 to 0.109375
- output_weight: bfloat16 [16, 128, 3072], P('seq', None, 'cand'), may hold values from -0.75 to 0.75
- cotangent: bfloat16 [4, 384, 3072], P('cand', 'seq'), may hold values from -6 to 6
Outputs:
- block_out: bfloat16 [4, 384, 3072], P('cand', 'seq')
- latent_grad: float32 [4, 384, 3072], P('cand', 'seq')
All inputs are finite; a program needn't handle non-finite values.
Results may differ from a plain program's by a relative error of at most 0.033.
Values may be sent and summed in bfloat16 or wider, within the bound.
A program may use at most 128 MiB of HBM per device.

v0:
```python
import jax
import jax.numpy as jnp
import numpy as np
from jax import lax
from jax.sharding import PartitionSpec as P

HEAD = 128
epsilon = 1e-06


def time_embed(timesteps, feature_width):
    half_size = feature_width // 2
    freq_rate = jnp.exp(-jnp.log(10000.0) * jnp.arange(half_size, dtype=jnp.float32) / half_size)
    angles = timesteps.astype(jnp.float32)[:, None] * freq_rate[None, :]
    return jnp.concatenate([jnp.cos(angles), jnp.sin(angles)], axis=1)


def rope_tables(positions, head_size):
    first_size = head_size // 8
    other_size = (head_size - first_size) // 2
    pieces = []
    swapped = []
    sign_vec = []
    offset = 0
    for axis_id, width_part in enumerate((first_size, other_size, other_size)):
        half_size = width_part // 2
        freq_rate = jnp.exp(
            -jnp.log(256.0) * 2.0 * jnp.arange(half_size, dtype=jnp.float32) / width_part
        )
        angle_part = positions[axis_id].astype(jnp.float32)[:, None] * freq_rate[None, :]
        pieces.append(angle_part)
        pieces.append(angle_part)
        swapped += list(range(offset + half_size, offset + width_part)) + list(
            range(offset, offset + half_size)
        )
        sign_vec += [-1.0] * half_size + [1.0] * half_size
        offset += width_part
    angles = jnp.concatenate(pieces, axis=1)
    return (
        jnp.cos(angles),
        jnp.sin(angles),
        np.array(swapped, np.int32),
        np.array(sign_vec, np.float32),
    )


def rotate(values, tables):
    cos_tab, sin_tab, swapped, sign_vec = tables
    return values * cos_tab + values[..., swapped] * sign_vec * sin_tab


def unrotate(values, tables):
    cos_tab, sin_tab, swapped, sign_vec = tables
    return values * cos_tab - (values * sin_tab)[..., swapped] * sign_vec


def rms_norm(values):
    inverse = lax.rsqrt(jnp.mean(values * values, -1, keepdims=True) + epsilon)
    return (values * inverse, inverse)


def rms_back(d_normed, normed, inverse):
    return inverse * (d_normed - normed * jnp.mean(d_normed * normed, -1, keepdims=True))


def layer_norm(values):
    centred = values - jnp.mean(values, -1, keepdims=True)
    inverse_std = lax.rsqrt(jnp.mean(centred * centred, -1, keepdims=True) + epsilon)
    return (centred * inverse_std, inverse_std)


def layer_norm_back(d_normed, normed, inverse_std):
    return inverse_std * (
        d_normed
        - jnp.mean(d_normed, -1, keepdims=True)
        - normed * jnp.mean(d_normed * normed, -1, keepdims=True)
    )


def times_transposed(left, right):
    return lax.dot_general(
        left, right, (((1,), (1,)), ((), ())), preferred_element_type=jnp.float32
    )


def attend(projected, tables):
    length, groups, triple = projected.shape
    head_size = triple // 3
    grouped = jnp.transpose(projected.reshape(length, groups, 3, head_size), (2, 1, 0, 3))
    query_n, query_inv = rms_norm(grouped[0])
    key_n, key_inv = rms_norm(grouped[1])
    q_rot = rotate(query_n, tables).astype(jnp.bfloat16)
    k_rot = rotate(key_n, tables).astype(jnp.bfloat16)
    values = grouped[2].astype(jnp.bfloat16)
    score_scale = head_size ** (-0.5)
    scores = (
        jnp.einsum("gld,gmd->glm", q_rot, k_rot, preferred_element_type=jnp.float32) * score_scale
    )
    weights = jnp.exp(scores - head_size**0.5)
    probs = weights / jnp.sum(weights, -1, keepdims=True)
    probs_low = probs.astype(jnp.bfloat16)
    heads_out = jnp.einsum("glm,gmd->gld", probs_low, values, preferred_element_type=jnp.float32)
    attended = (
        jnp.transpose(heads_out, (1, 0, 2)).reshape(length, groups * head_size).astype(jnp.bfloat16)
    )
    saved = (q_rot, k_rot, values, probs, probs_low, query_n, query_inv, key_n, key_inv)
    return (attended, saved)


def attend_back(d_attended, saved, tables):
    q_rot, k_rot, values, probs, probs_low, query_n, query_inv, key_n, key_inv = saved
    groups, length, head_size = q_rot.shape
    score_scale = head_size ** (-0.5)
    d_heads = jnp.transpose(d_attended.reshape(length, groups, head_size), (1, 0, 2))
    d_values = jnp.einsum("glm,gld->gmd", probs_low, d_heads, preferred_element_type=jnp.float32)
    d_probs = jnp.einsum("gld,gmd->glm", d_heads, values, preferred_element_type=jnp.float32)
    d_scores = (probs * (d_probs - jnp.sum(probs * d_probs, -1, keepdims=True))).astype(
        jnp.bfloat16
    )
    d_qrot = (
        jnp.einsum("glm,gmd->gld", d_scores, k_rot, preferred_element_type=jnp.float32)
        * score_scale
    )
    d_krot = (
        jnp.einsum("glm,gld->gmd", d_scores, q_rot, preferred_element_type=jnp.float32)
        * score_scale
    )
    d_query = rms_back(unrotate(d_qrot, tables), query_n, query_inv)
    d_key = rms_back(unrotate(d_krot, tables), key_n, key_inv)
    stacked = jnp.stack([d_query, d_key, d_values], 0)
    return (
        jnp.transpose(stacked, (2, 1, 0, 3))
        .reshape(length, groups * 3 * head_size)
        .astype(jnp.bfloat16)
    )


def on_device(latent, timesteps, positions, mod_weight, input_weight, output_weight, cotangent):
    width = latent.shape[2]
    rows_local = latent.shape[1]
    groups = input_weight.shape[1]
    group_cols = groups * input_weight.shape[2]
    time_act = jax.nn.silu(time_embed(timesteps, width)).astype(jnp.bfloat16)
    slab_rows = mod_weight.shape[0]
    act_rows = lax.dynamic_slice_in_dim(time_act, lax.axis_index("cand") * slab_rows, slab_rows, 1)
    mod_mine = lax.psum_scatter(
        jnp.dot(act_rows, mod_weight, preferred_element_type=jnp.float32).astype(jnp.bfloat16),
        "cand",
        scatter_dimension=0,
        tiled=True,
    ).astype(jnp.float32)
    modulation = lax.all_gather(mod_mine, "seq", axis=1, tiled=True)[0]
    shift_vec = modulation[:width]
    scale_vec = modulation[width : 2 * width]
    gate_vec = modulation[2 * width :]
    latent_rows = latent[0].astype(jnp.float32)
    normed, inverse_std = layer_norm(latent_rows)
    modulated = (normed * (1.0 + scale_vec) + shift_vec).astype(jnp.bfloat16)
    gathered = lax.all_gather(modulated, "seq", axis=0, tiled=True)
    length = gathered.shape[0]
    tables = rope_tables(positions, HEAD)
    piece = lax.all_gather(input_weight, "cand", axis=0, tiled=True)
    projected = jnp.dot(
        gathered, piece.reshape(piece.shape[0], group_cols), preferred_element_type=jnp.float32
    )
    attended, saved = attend(projected.reshape(length, groups, 3 * HEAD), tables)
    w_heads = lax.all_gather(output_weight, "seq", axis=0, tiled=True)
    w_all = lax.all_gather(w_heads, "cand", axis=2, tiled=True)
    w_all = w_all.reshape(w_all.shape[0] * w_all.shape[1], width)
    token_heads = lax.all_to_all(attended, "seq", split_axis=0, concat_axis=1, tiled=True)
    mixed = jnp.dot(token_heads, w_all, preferred_element_type=jnp.float32)
    block_out = (latent_rows + gate_vec * mixed).astype(jnp.bfloat16)
    d_mixed = (cotangent[0].astype(jnp.float32) * gate_vec).astype(jnp.bfloat16)
    d_tokens = times_transposed(d_mixed, w_all).astype(jnp.bfloat16)
    d_attended = lax.all_to_all(d_tokens, "seq", split_axis=1, concat_axis=0, tiled=True)
    d_projected = attend_back(d_attended, saved, tables)
    w_back = lax.all_gather(input_weight, "cand", axis=0, tiled=True).reshape(width, group_cols)
    d_modulated = lax.psum_scatter(
        times_transposed(
            lax.slice_in_dim(d_projected, 0, rows_local * lax.axis_size("seq"), axis=0), w_back
        ).astype(jnp.bfloat16),
        "seq",
        scatter_dimension=0,
        tiled=True,
    ).astype(jnp.float32)
    latent_grad = cotangent[0].astype(jnp.float32) + layer_norm_back(
        d_modulated * (1.0 + scale_vec), normed, inverse_std
    )
    return (block_out[None], latent_grad[None])


def solution(mesh):
    placed = (
        P("cand", "seq", None),
        P(),
        P(),
        P("cand", "seq"),
        P("cand", "seq", None),
        P("seq", None, "cand"),
        P("cand", "seq", None),
    )
    return jax.shard_map(
        on_device,
        mesh=mesh,
        in_specs=placed,
        out_specs=(P("cand", "seq", None), P("cand", "seq", None)),
        check_vma=False,
    )
```

profile of v0, /device:TPU:0, one launch (start us, length us, event | category | flops | bytes accessed | tf_op | source)
XLA Modules:
  0.0 380.3 jit_solution(16041550091423698796)
XLA Ops:
  7.2 0.7 all-gather.9.cloned.1.call-update
  8.0 0.7 all-gather.7.cloned.1.call-update
  8.8 0.6 dynamic-slice
  9.7 0.3 convolution_convert_fusion.2
  10.0 8.7 %all-reduce = bf16[4,1152]{1,0:T(4,128)(2,1)S(1)} all-reduce(bf16[4,1152]{1,0:T(4,128)(2,1)S(1)} %convolution_convert_fusion.2), channel_id=2, replica_groups=mesh['cand'=4,'seq'=8] {'cand'}, use_global_device_ids=true, to_apply=%region_0.1.clone | all-reduce | flops 4608 | bytes 18432
  18.7 0.7 dynamic-slice_convert_fusion
  19.4 31.6 %all_gather.16 = f32[1,9216]{1,0:T(1,128)S(1)} all-gather(f32[1,1152]{1,0:T(1,128)S(1)} %dynamic-slice_convert_fusion), channel_id=1, replica_groups=mesh['cand'=4,'seq'=8] {'seq'}, dimensions={1}, use_global_device_ids=true | all-gather | bytes 41472 | tf_op jit(solution)/shard_map/all_gather | solution.py:152
  51.4 0.9 fusion.19
  52.4 20.8 %all-gather.9.cloned.1.call-done = bf16[16,128,768]{2,1,0:T(8,128)(2,1)} async-done(((bf16[2,128,768]{2,1,0:T(8,128)(2,1)}), bf16[16,128,768]{2,1,0:T(8,128)(2,1)}) %all-gather.9.cloned.1.call-update) | async-done | bytes 3145744 | tf_op jit(solution)/shard_map/all_gather | solution.py:167
  73.2 0.6 copy-done.25
  74.4 0.6 pad_clamp_fusion
  74.9 0.7 fusion.61
  75.6 0.8 broadcast_multiply_fusion.2
  76.4 34.5 %all-gather.7.cloned.1.call-done = bf16[3072,2,384]{2,1,0:T(2,128)(2,1)} async-done(((bf16[768,2,384]{2,1,0:T(2,128)(2,1)}), bf16[3072,2,384]{2,1,0:T(2,128)(2,1)}) %all-gather.7.cloned.1.call-update) | async-done | bytes 4718608 | tf_op jit(solution)/shard_map/all_gather | solution.py:162
  110.9 5.2 %copy.89 = bf16[384,8,2,384]{3,1,2,0:T(8,128)(2,1)} copy(bf16[384,8,2,384]{3,2,1,0:T(2,128)(2,1)} %bitcast.149) | data formatting | bytes 9437184
  116.1 6.7 %copy.50 = bf16[3072,768]{0,1:T(8,128)(2,1)} copy(bf16[3072,768]{1,0:T(8,128)(2,1)} %bitcast.145) | data formatting | bytes 9437184 | tf_op jit(solution)/shard_map/reshape | solution.py:164
  122.8 42.7 %all-gather.5.cloned.1.call-done = bf16[384,3072]{1,0:T(8,128)(2,1)} async-done(((bf16[48,3072]{1,0:T(8,128)(2,1)}), bf16[384,3072]{1,0:T(8,128)(2,1)}) %all-gather.5.cloned.1.call-update) | async-done | bytes 2359312 | tf_op jit(solution)/shard_map/all_gather | solution.py:159
  165.5 5.3 %fusion.5 = f32[3,2,384,128]{2,3,0,1:T(8,128)S(1)} fusion(bf16[2,3,128,3072]{3,2,1,0:T(8,128)(2,1)} %bitcast.150, bf16[384,3072]{1,0:T(8,128)(2,1)} %all-gather.5.cloned.1.call-done), kind=kOutput, calls=%fused_computation.13 | convolution fusion | flops 1811939328 | bytes 8257536 | tf_op jit(solution)/shard_map/dot_general | solution.py:163
  170.8 1.0 copy-done.6
  171.9 75.6 %all-gather.11.cloned.1.call-done = bf16[16,128,3072]{2,1,0:T(8,128)(2,1)} async-done(((bf16[16,128,768]{2,1,0:T(8,128)(2,1)}), bf16[16,128,3072]{2,1,0:T(8,128)(2,1)}) %all-gather.11.cloned.1.call-update) | async-done | bytes 12582928 | tf_op jit(solution)/shard_map/all_gather | solution.py:168
  247.6 8.5 %convolution_convert_fusion.1 = bf16[48,2048]{1,0:T(8,128)(2,1)S(1)} fusion(bf16[2048,3072]{1,0:T(8,128)(2,1)} %bitcast.143, bf16[1,48,3072]{2,1,0:T(8,128)(2,1)S(1)} %copy-done.10, f32[3072]{0:T(1024)S(1)} %bitcast.159), kind=kOutput, calls=%fused_computation.11 | convolution fusion | flops 604520448 | bytes 13086720 | tf_op jit(solution)/shard_map/dot_general | solution.py:81
  256.0 0.7 copy.119
  256.7 5.5 %all-to-all-start.1 = ((bf16[48,8,256]{2,0,1:T(8,128)(2,1)}), bf16[48,8,256]{2,0,1:T(8,128)(2,1)S(1)}, u32[]{:S(2)}, u32[]{:S(2)}) async-start(bf16[48,8,256]{2,0,1:T(8,128)(2,1)} %bitcast.142), calls=%async_computation.1 | async-start | bytes 393216 | tf_op jit(solution)/shard_map/all_to_all | solution.py:175
  262.5 1.2 fusion.35
  263.7 1.1 copy.52
  264.8 1.0 copy.54
  265.8 2.2 gather_fusion
  268.0 2.9 gather_fusion.1
  270.9 1.9 fusion.31
  272.9 2.5 fusion.45
  275.3 2.1 multiply_reduce_fusion
  277.5 1.1 fusion.11
  278.9 0.8 copy-done.14
  280.0 0.6 copy-done.13
  280.7 1.1 broadcast_multiply_fusion
  281.8 1.0 copy.69
  282.8 2.9 gather_fusion.3
  285.7 2.0 copy.66
  287.8 2.9 gather_fusion.2
  290.6 2.0 multiply_reduce_fusion.2
  292.7 2.0 fusion.41
  294.9 3.5 convolution_convert_fusion
  298.4 1.4 fusion.10
  300.2 18.7 %all_to_all.32 = bf16[8,48,256]{2,1,0:T(8,128)(2,1)S(1)} all-to-all(bf16[8,48,256]{2,1,0:T(8,128)(2,1)S(1)} %convert_element_type.131), channel_id=1, replica_groups=mesh['cand'=4,'seq'=8] {'seq'}, dimensions={0} | all-to-all | bytes 393216 | tf_op jit(solution)/shard_map/all_to_all | solution.py:170
  319.0 7.9 %fusion.2 = bf16[1,48,3072]{2,1,0:T(8,128)(2,1)} fusion(bf16[48,2048]{1,0:T(8,128)(2,1)S(1)} %bitcast.151, bf16[2048,3072]{1,0:T(8,128)(2,1)} %bitcast.144, bf16[1,48,3072]{2,1,0:T(8,128)(2,1)S(1)} %copy-done.2, f32[3072]{0:T(1024)S(1)} %bitcast.160), kind=kOutput, calls=%fused_computation.8 | convolution fusion | flops 604569600 | bytes 13381632 | tf_op jit(solution)/shard_map/dot_general | solution.py:171
  326.9 43.6 %reduce-scatter.2.cloned.1.call-done = bf16[48,3072]{1,0:T(8,128)(2,1)} async-done(((bf16[384,3072]{1,0:T(8,128)(2,1)}), bf16[48,3072]{1,0:T(8,128)(2,1)}) %reduce-scatter.2.cloned.1.call-update) | async-done | bytes 294928 | tf_op jit(solution)/shard_map/reduce_scatter | solution.py:178
  370.5 1.2 fusion.27
  371.8 2.0 fusion.24
  (96 shorter events, 3.1 us)
Async XLA Ops:
  7.2 2.5 copy-start
  7.2 1.6 copy-start.28
  7.2 1.6 copy-start.27
  7.2 66.0 %all-gather.9.cloned.1.call-start = ((), (), s32[]{:S(2)}) async-start(), calls=%async_computation.5 | async-start | bytes 3538944 | tf_op jit(solution)/shard_map/all_gather | solution.py:167
  7.9 103.0 %all-gather.7.cloned.1.call-start = ((), (), s32[]{:S(2)}) async-start(), calls=%async_computation.4 | async-start | bytes 5898240 | tf_op jit(solution)/shard_map/all_gather | solution.py:162
  8.7 42.3 %copy-start.1 = (bf16[1,48,3072]{2,1,0:T(8,128)(2,1)S(1)}, bf16[1,48,3072]{2,1,0:T(8,128)(2,1)}, u32[]{:S(2)}) copy-start(bf16[1,48,3072]{2,1,0:T(8,128)(2,1)} %param.13) | copy-start | bytes 884740
  8.7 156.8 %all-gather.5.cloned.1.call-start = ((), (), s32[]{:S(2)}) async-start(), calls=%async_computation.3 | async-start | bytes 2654208 | tf_op jit(solution)/shard_map/all_gather | solution.py:159
  51.1 22.1 %copy-start.20 = (f32[48]{0:T(128)}, f32[48]{0:T(128)S(1)}, u32[]{:S(2)}) copy-start(f32[48]{0:T(128)S(1)} %broadcast_multiply_fusion.11) | copy-start | bytes 580
  51.4 21.8 %copy-start.23 = (f32[48]{0:T(128)}, f32[48]{0:T(128)S(1)}, u32[]{:S(2)}) copy-start(f32[48]{0:T(128)S(1)} %add_rsqrt_fusion.2) | copy-start | bytes 580
  51.4 196.1 %copy-start.16 = (f32[1,3072]{1,0:T(1,128)}, f32[1,3072]{1,0:T(1,128)S(1)}, u32[]{:S(2)}) copy-start(f32[1,3072]{1,0:T(1,128)S(1)} %get-tuple-element.21) | copy-start | bytes 36868
  52.4 195.2 %all-gather.11.cloned.1.call-start = ((), (), s32[]{:S(2)}) async-start(), calls=%async_computation.6 | async-start | bytes 15728640 | tf_op jit(solution)/shard_map/all_gather | solution.py:168
  73.2 0.7 copy-start.25
  73.2 1.2 copy-start.26
  165.5 82.1 %copy-start.10 = (bf16[1,48,3072]{2,1,0:T(8,128)(2,1)S(1)}, bf16[1,48,3072]{2,1,0:T(8,128)(2,1)}, u32[]{:S(2)}) copy-start(bf16[1,48,3072]{2,1,0:T(8,128)(2,1)} %param.19) | copy-start | bytes 884740
  170.8 1.1 copy-start.6
  171.9 90.5 %copy-start.18 = (f32[2,384]{1,0:T(2,128)}, f32[2,384]{1,0:T(2,128)S(1)}, u32[]{:S(2)}) copy-start(f32[2,384]{1,0:T(2,128)S(1)} %get-tuple-element.32) | copy-start | bytes 9220
  256.7 16.1 %all-to-all-start.1 = ((bf16[48,8,256]{2,0,1:T(8,128)(2,1)}), bf16[48,8,256]{2,0,1:T(8,128)(2,1)S(1)}, u32[]{:S(2)}, u32[]{:S(2)}) async-start(bf16[48,8,256]{2,0,1:T(8,128)(2,1)} %bitcast.142), calls=%async_computation.1 | async-start | bytes 393216 | tf_op jit(solution)/shard_map/all_to_all | solution.py:175
  262.2 108.2 %reduce-scatter.2.cloned.1.call-start = ((), (), s32[]{:S(2)}) async-start(), calls=%async_computation.7 | async-start | bytes 2654208 | tf_op jit(solution)/shard_map/reduce_scatter | solution.py:178
  263.7 11.7 %copy-start.3 = (f32[2,384,128]{1,2,0:T(8,128)}, f32[2,384,128]{1,2,0:T(8,128)S(1)}, u32[]{:S(2)}) copy-start(f32[2,384,128]{1,2,0:T(8,128)S(1)} %get-tuple-element.11) | copy-start | bytes 1179652
  263.7 11.7 %copy-start.4 = (f32[2,384,128]{1,2,0:T(8,128)}, f32[2,384,128]{1,2,0:T(8,128)S(1)}, u32[]{:S(2)}) copy-start(f32[2,384,128]{1,2,0:T(8,128)S(1)} %get-tuple-element.12) | copy-start | bytes 1179652
  272.8 2.5 copy-start.8
  275.3 2.1 copy-start.9
  277.5 1.3 copy-start.7
  278.7 0.9 copy-start.14
  279.7 0.9 copy-start.13
  279.7 1.0 copy-start.15
  279.9 1.9 copy-start.5
  281.8 13.1 %slice-start = ((s8[4718592]{0:T(1024)(128)(4,1)}), s8[524288]{0:T(1024)(128)(4,1)S(1)}, s32[]{:S(2)}) async-start(s8[4718592]{0:T(1024)(128)(4,1)} %bitcast.146), calls=%async_computation.8 | async-start | bytes 1048576
  282.8 7.8 %copy-start.22 = (f32[128]{0:T(128)S(1)}, f32[128]{0:T(128)}, u32[]{:S(2)}) copy-start(f32[128]{0:T(128)} %constant.63.clone) | copy-start | bytes 1540
  287.8 4.9 %copy-start.19 = (f32[2,384]{1,0:T(2,128)S(1)}, f32[2,384]{1,0:T(2,128)}, u32[]{:S(2)}) copy-start(f32[2,384]{1,0:T(2,128)} %copy-done.18) | copy-start | bytes 9220
  290.6 4.2 %slice-start.1 = ((s8[4718592]{0:T(1024)(128)(4,1)}), s8[4194304]{0:T(1024)(128)(4,1)S(1)}, s32[]{:S(2)}) async-start(s8[4718592]{0:T(1024)(128)(4,1)} %bitcast.146), calls=%async_computation.9 | async-start | bytes 8388608
  292.7 2.0 copy-start.12
  299.8 19.1 %copy-start.2 = (bf16[1,48,3072]{2,1,0:T(8,128)(2,1)S(1)}, bf16[1,48,3072]{2,1,0:T(8,128)(2,1)}, u32[]{:S(2)}) copy-start(bf16[1,48,3072]{2,1,0:T(8,128)(2,1)} %param.13) | copy-start | bytes 884740
  299.8 19.1 %copy-start.17 = (f32[1,3072]{1,0:T(1,128)S(1)}, f32[1,3072]{1,0:T(1,128)}, u32[]{:S(2)}) copy-start(f32[1,3072]{1,0:T(1,128)} %copy-done.16) | copy-start | bytes 36868
  318.9 51.6 %copy-start.21 = (f32[48]{0:T(128)S(1)}, f32[48]{0:T(128)}, u32[]{:S(2)}) copy-start(f32[48]{0:T(128)} %copy-done.20) | copy-start | bytes 580
  318.9 51.6 %copy-start.24 = (f32[48]{0:T(128)S(1)}, f32[48]{0:T(128)}, u32[]{:S(2)}) copy-start(f32[48]{0:T(128)} %copy-done.23) | copy-start | bytes 580
  318.9 52.8 %copy-start.11 = (bf16[1,48,3072]{2,1,0:T(8,128)(2,1)S(1)}, bf16[1,48,3072]{2,1,0:T(8,128)(2,1)}, u32[]{:S(2)}) copy-start(bf16[1,48,3072]{2,1,0:T(8,128)(2,1)} %param.19) | copy-start | bytes 884740
Sparse Core Ops, SparseCore 0:
  10.2 62.9 all-gather.8
  74.7 36.1 all-gather.6
  113.7 51.8 all-gather.4
  166.9 80.6 all-gather.10
  298.5 71.9 reduce-scatter.1
where the time goes:
time: 381 us; the launch traced here: 380 us
  waiting for transfers between devices  219 us (57%)
  blocking collectives  59 us (15%)
  local copies, waits for them, and re-layouts  34.1 us (9%)
  matrix products  33.8 us (9%)
  other arithmetic  14.5 us (4%)
  between operations  14.3 us (4%)
  starting transfers between devices  5.89 us (2%)
    all_gather x1, waiting for transfers between devices, on_device(): w_all = lax.all_gather(w_heads, 'cand', axis=2, tiled=True)  75.6 us
    reduce_scatter x1, waiting for transfers between devices, on_device(): lax.psum_scatter(times_transposed(lax.slice_in_dim(d_projected, 0, rows_l...  43.6 us
    all_gather x1, waiting for transfers between devices, on_device(): gathered = lax.all_gather(modulated, 'seq', axis=0, tiled=True)  42.7 us
    all_gather x1, waiting for transfers between devices, on_device(): piece = lax.all_gather(input_weight, 'cand', axis=0, tiled=True)  34.5 us
    all_gather x1, blocking collectives, on_device(): modulation = lax.all_gather(mod_mine, 'seq', axis=1, tiled=True)[0]  31.6 us
    all_gather x1, waiting for transfers between devices, on_device(): w_heads = lax.all_gather(output_weight, 'seq', axis=0, tiled=True)  20.8 us
    all_to_all x1, blocking collectives, on_device(): lax.all_to_all(attended, 'seq', split_axis=0, concat_axis=1, tiled=True)  18.7 us
    dot_general x2, matrix products, times_transposed(): lax.dot_general(left, right, (((1,), (1,)), ((), ())), preferred_element_...  11.9 us
  transfers between devices with their start and end apart: 6, of which 5 were waited for; matrix products, arithmetic and copies ran while one was open for 11% of the time, Pallas kernels for 0%

commit v1 on v0

--- a/solution.py
+++ b/solution.py
@@ -159,7 +159,9 @@
     gathered = lax.all_gather(modulated, "seq", axis=0, tiled=True)
     length = gathered.shape[0]
     tables = rope_tables(positions, HEAD)
-    piece = lax.all_gather(input_weight, "cand", axis=0, tiled=True)
+    piece = jnp.concatenate(
+        lax.all_to_all(jnp.stack([input_weight] * lax.axis_size("cand")), "cand", 0, 0), axis=0
+    )
     projected = jnp.dot(
         gathered, piece.reshape(piece.shape[0], group_cols), preferred_element_type=jnp.float32
     )

time: 381 us -> 362 us (0.950)
  waiting for transfers between devices: 219 us -> 173 us
  local copies, waits for them, and re-layouts: 34.1 us -> 56.6 us
  starting transfers between devices: 5.89 us -> 11 us
    all_to_all x0 -> x1, waiting for transfers between devices: none -> 51.8 us  [on_device(): lax.all_to_all(jnp.stack([input_weight] * lax.axis_size('cand')), 'cand',...]
    all_gather x1, waiting for transfers between devices: 42.7 us -> 0.01 us  [on_device(): gathered = lax.all_gather(modulated, 'seq', axis=0, tiled=True)]
    all_gather x1, waiting for transfers between devices: 75.6 us -> 40.6 us  [on_device(): w_all = lax.all_gather(w_heads, 'cand', axis=2, tiled=True)]
    all_gather x1, waiting for transfers between devices: 34.5 us -> 15.2 us  [on_device(): lax.all_gather(input_weight, 'cand', axis=0, tiled=True)]
    all_to_all x0 -> x1, local copies, waits for them, and re-layouts: none -> 12.7 us  [on_device(): lax.all_to_all(jnp.stack([input_weight] * lax.axis_size('cand')), 'cand',...]
    unnamed x64 -> x40, local copies, waits for them, and re-layouts: 9.31 us -> 16.1 us
    reshape x1 -> x0, local copies, waits for them, and re-layouts: 6.68 us -> none  [on_device(): piece.reshape(piece.shape[0], group_cols)]
    dot_general x0 -> x1, local copies, waits for them, and re-layouts: none -> 6.6 us  [on_device(): jnp.dot(gathered, piece.reshape(piece.shape[0], group_cols), preferred_el...]
  transfers between devices with their start and end apart: 6 -> 7, of which waited for: 5 -> 5; matrix products, arithmetic and copies ran while one was open for 11% -> 20% of each run, Pallas kernels for 0% -> 0%
where the time goes in v1:
time: 362 us; the launch traced here: 360 us
  waiting for transfers between devices  173 us (48%)
  blocking collectives  58.9 us (16%)
  local copies, waits for them, and re-layouts  56.6 us (16%)
  matrix products  35 us (10%)
  between operations  14.1 us (4%)
  starting transfers between devices  11 us (3%)
  other arithmetic  11 us (3%)
    all_to_all x1, waiting for transfers between devices, on_device(): lax.all_to_all(jnp.stack([input_weight] * lax.axis_size('cand')), 'cand',...  51.8 us
    reduce_scatter x1, waiting for transfers between devices, on_device(): lax.psum_scatter(times_transposed(lax.slice_in_dim(d_projected, 0, rows_l...  44.1 us
    all_gather x1, waiting for transfers between devices, on_device(): w_all = lax.all_gather(w_heads, 'cand', axis=2, tiled=True)  40.6 us
    all_gather x1, blocking collectives, on_device(): modulation = lax.all_gather(mod_mine, 'seq', axis=1, tiled=True)[0]  31.6 us
    all_gather x1, waiting for transfers between devices, on_device(): w_heads = lax.all_gather(output_weight, 'seq', axis=0, tiled=True)  20.4 us
    all_to_all x1, blocking collectives, on_device(): lax.all_to_all(attended, 'seq', split_axis=0, concat_axis=1, tiled=True)  18.6 us
    unnamed x40, local copies, waits for them, and re-layouts  16.1 us
    all_gather x1, waiting for transfers between devices, on_device(): lax.all_gather(input_weight, 'cand', axis=0, tiled=True)  15.2 us
  transfers between devices with their start and end apart: 7, of which 5 were waited for; matrix products, arithmetic and copies ran while one was open for 20% of the time, Pallas kernels for 0%

profile of v1, /device:TPU:0, one launch (start us, length us, event | category | flops | bytes accessed | tf_op | source)
XLA Modules:
  0.0 360.1 jit_solution(8589201587457308293)
XLA Ops:
  7.2 0.7 all-gather.7.cloned.1.call-update
  8.0 0.7 convert_element_type.114
  8.6 1.2 dynamic-slice
  10.5 8.7 %all-reduce = bf16[4,1152]{1,0:T(4,128)(2,1)S(1)} all-reduce(bf16[4,1152]{1,0:T(4,128)(2,1)S(1)} %convolution_convert_fusion.2), channel_id=2, replica_groups=mesh['cand'=4,'seq'=8] {'cand'}, use_global_device_ids=true, to_apply=%region_0.1.clone | all-reduce | flops 4608 | bytes 18432
  19.2 0.7 dynamic-slice_convert_fusion
  19.9 31.6 %all_gather.15 = f32[1,9216]{1,0:T(1,128)S(1)} all-gather(f32[1,1152]{1,0:T(1,128)S(1)} %dynamic-slice_convert_fusion), channel_id=1, replica_groups=mesh['cand'=4,'seq'=8] {'seq'}, dimensions={1}, use_global_device_ids=true | all-gather | bytes 41472 | tf_op jit(solution)/shard_map/all_gather | solution.py:152
  51.9 0.9 fusion.19
  52.8 20.4 %all-gather.7.cloned.1.call-done = bf16[16,128,768]{2,1,0:T(8,128)(2,1)} async-done(((bf16[2,128,768]{2,1,0:T(8,128)(2,1)}), bf16[16,128,768]{2,1,0:T(8,128)(2,1)}) %all-gather.7.cloned.1.call-update) | async-done | bytes 3145744 | tf_op jit(solution)/shard_map/all_gather | solution.py:169
  73.9 0.7 copy-done.5
  74.6 2.0 copy.74
  76.6 2.5 stack.23
  79.0 5.1 %all-to-all-start = ((bf16[4,768,2,384]{1,3,2,0:T(8,128)(2,1)}), bf16[4,768,2,384]{1,3,2,0:T(8,128)(2,1)}, u32[]{:S(2)}, u32[]{:S(2)}) async-start(bf16[4,768,2,384]{1,3,2,0:T(8,128)(2,1)} %stack.23), calls=%async_computation | async-start | bytes 9437184 | tf_op jit(solution)/shard_map/all_to_all | solution.py:163
  84.8 0.7 fusion.61
  85.5 0.7 broadcast_multiply_fusion.2
  86.2 51.8 %all-to-all-done = bf16[4,768,2,384]{1,3,2,0:T(8,128)(2,1)} async-done(((bf16[4,768,2,384]{1,3,2,0:T(8,128)(2,1)}), bf16[4,768,2,384]{1,3,2,0:T(8,128)(2,1)}, u32[]{:S(2)}, u32[]{:S(2)}) %all-to-all-start) | async-done | bytes 4718624 | tf_op jit(solution)/shard_map/all_to_all | solution.py:163
  138.0 12.7 %copy.75 = bf16[4,768,2,384]{3,2,1,0:T(2,128)(2,1)} copy(bf16[4,768,2,384]{1,3,2,0:T(8,128)(2,1)} %all-to-all-done) | data formatting | bytes 9437184 | tf_op jit(solution)/shard_map/all_to_all | solution.py:163
  150.7 5.3 %copy.115 = bf16[384,8,2,384]{3,1,2,0:T(8,128)(2,1)} copy(bf16[384,8,2,384]{3,2,1,0:T(2,128)(2,1)} %bitcast.148) | data formatting | bytes 9437184
  156.0 6.6 %copy.76 = bf16[768,3072]{1,0:T(8,128)(2,1)} copy(bf16[768,3072]{0,1:T(8,128)(2,1)} %bitcast.149) | data formatting | bytes 9437184 | tf_op jit(solution)/shard_map/dot_general | solution.py:165
  162.6 5.3 %fusion.5 = f32[3,2,384,128]{2,3,0,1:T(8,128)S(1)} fusion(bf16[2,3,128,3072]{3,2,1,0:T(8,128)(2,1)} %bitcast.152, bf16[384,3072]{1,0:T(8,128)(2,1)} %all-gather.5.cloned.1.call-done), kind=kOutput, calls=%fused_computation.13 | convolution fusion | flops 1811939328 | bytes 8257536 | tf_op jit(solution)/shard_map/dot_general | solution.py:165
  168.0 40.6 %all-gather.9.cloned.1.call-done = bf16[16,128,3072]{2,1,0:T(8,128)(2,1)} async-done(((bf16[16,128,768]{2,1,0:T(8,128)(2,1)}), bf16[16,128,3072]{2,1,0:T(8,128)(2,1)}) %all-gather.9.cloned.1.call-update) | async-done | bytes 12582928 | tf_op jit(solution)/shard_map/all_gather | solution.py:170
  208.6 8.5 %convolution_convert_fusion.1 = bf16[48,2048]{1,0:T(8,128)(2,1)S(1)} fusion(bf16[2048,3072]{1,0:T(8,128)(2,1)} %bitcast.146, bf16[1,48,3072]{2,1,0:T(8,128)(2,1)S(1)} %copy-done.8, f32[3072]{0:T(1024)S(1)} %bitcast.160), kind=kOutput, calls=%fused_computation.11 | convolution fusion | flops 604520448 | bytes 13086720 | tf_op jit(solution)/shard_map/dot_general | solution.py:81
  217.1 0.7 copy.146
  217.8 5.5 %all-to-all-start.2 = ((bf16[48,8,256]{2,0,1:T(8,128)(2,1)}), bf16[48,8,256]{2,0,1:T(8,128)(2,1)}, u32[]{:S(2)}, u32[]{:S(2)}) async-start(bf16[48,8,256]{2,0,1:T(8,128)(2,1)} %bitcast.145), calls=%async_computation.2 | async-start | bytes 393216 | tf_op jit(solution)/shard_map/all_to_all | solution.py:177
  223.6 1.1 copy.80
  224.6 1.1 copy.78
  225.7 2.0 gather_fusion.1
  227.7 2.8 gather_fusion
  230.5 1.8 fusion.31
  232.3 15.2 %all-gather.11.cloned.1.call-done = bf16[3072,2,384]{2,1,0:T(2,128)(2,1)} async-done(((bf16[768,2,384]{2,1,0:T(2,128)(2,1)}), bf16[3072,2,384]{2,1,0:T(2,128)(2,1)}) %all-gather.11.cloned.1.call-update) | async-done | bytes 4718608 | tf_op jit(solution)/shard_map/all_gather | solution.py:179
  247.5 5.3 %copy.116 = bf16[384,8,2,384]{3,1,2,0:T(8,128)(2,1)} copy(bf16[384,8,2,384]{3,2,1,0:T(2,128)(2,1)} %bitcast.150) | data formatting | bytes 9437184
  252.8 1.0 reshape.281
  253.8 1.5 fusion.45
  255.3 1.9 multiply_reduce_fusion
  257.2 1.1 fusion.11
  259.6 1.1 broadcast_multiply_fusion
  260.7 1.1 copy.92
  261.8 2.7 gather_fusion.2
  264.5 2.1 copy.95
  266.6 2.7 gather_fusion.3
  269.4 1.4 multiply_reduce_fusion.2
  271.1 0.7 copy-done.10
  271.9 5.8 %convolution_convert_fusion = bf16[384,3072]{1,0:T(8,128)(2,1)} fusion(bf16[384,768]{0,1:T(8,128)(2,1)S(1)} %bitcast.156, bf16[3072,768]{1,0:T(8,128)(2,1)} %bitcast.151), kind=kOutput, calls=%fused_computation.4 | convolution fusion | flops 1813118976 | bytes 7667712 | tf_op jit(solution)/shard_map/dot_general | solution.py:81
  277.8 1.4 fusion.10
  279.5 18.6 %all_to_all.37 = bf16[8,48,256]{2,1,0:T(8,128)(2,1)S(1)} all-to-all(bf16[8,48,256]{2,1,0:T(8,128)(2,1)S(1)} %convert_element_type.131), channel_id=1, replica_groups=mesh['cand'=4,'seq'=8] {'seq'}, dimensions={0} | all-to-all | bytes 393216 | tf_op jit(solution)/shard_map/all_to_all | solution.py:172
  298.2 8.0 %fusion.2 = bf16[1,48,3072]{2,1,0:T(8,128)(2,1)} fusion(bf16[48,2048]{1,0:T(8,128)(2,1)S(1)} %bitcast.153, bf16[2048,3072]{1,0:T(8,128)(2,1)} %bitcast.147, bf16[1,48,3072]{2,1,0:T(8,128)(2,1)S(1)} %copy-done.2, f32[3072]{0:T(1024)S(1)} %bitcast.161), kind=kOutput, calls=%fused_computation.8 | convolution fusion | flops 604569600 | bytes 13381632 | tf_op jit(solution)/shard_map/dot_general | solution.py:173
  306.2 44.1 %reduce-scatter.2.cloned.1.call-done = bf16[48,3072]{1,0:T(8,128)(2,1)} async-done(((bf16[384,3072]{1,0:T(8,128)(2,1)}), bf16[48,3072]{1,0:T(8,128)(2,1)}) %reduce-scatter.2.cloned.1.call-update) | async-done | bytes 294928 | tf_op jit(solution)/shard_map/reduce_scatter | solution.py:180
  350.2 1.2 fusion.27
  351.5 2.0 fusion.24
  (75 shorter events, 4.9 us)
Async XLA Ops:
  7.2 3.0 copy-start
  7.2 44.2 %copy-start.2 = (bf16[1,48,3072]{2,1,0:T(8,128)(2,1)S(1)}, bf16[1,48,3072]{2,1,0:T(8,128)(2,1)}, u32[]{:S(2)}) copy-start(bf16[1,48,3072]{2,1,0:T(8,128)(2,1)} %param.13) | copy-start | bytes 884740
  7.2 66.1 %all-gather.7.cloned.1.call-start = ((), (), s32[]{:S(2)}) async-start(), calls=%async_computation.5 | async-start | bytes 3538944 | tf_op jit(solution)/shard_map/all_gather | solution.py:169
  7.9 154.7 %all-gather.5.cloned.1.call-start = ((), (), s32[]{:S(2)}) async-start(), calls=%async_computation.4 | async-start | bytes 2654208 | tf_op jit(solution)/shard_map/all_gather | solution.py:159
  52.8 155.8 %all-gather.9.cloned.1.call-start = ((), (), s32[]{:S(2)}) async-start(), calls=%async_computation.6 | async-start | bytes 15728640 | tf_op jit(solution)/shard_map/all_gather | solution.py:170
  73.3 1.3 copy-start.5
  73.3 174.2 %all-gather.11.cloned.1.call-start = ((), (), s32[]{:S(2)}) async-start(), calls=%async_computation.7 | async-start | bytes 5898240 | tf_op jit(solution)/shard_map/all_gather | solution.py:179
  79.0 5.2 %copy-start.16 = (s32[3,384]{1,0:T(4,128)S(1)}, s32[3,384]{1,0:T(4,128)}, u32[]{:S(2)}) copy-start(s32[3,384]{1,0:T(4,128)} %param.15) | copy-start | bytes 13828
  79.0 5.7 %copy-start.17 = (s32[128]{0:T(128)S(1)}, s32[128]{0:T(128)}, u32[]{:S(2)}) copy-start(s32[128]{0:T(128)} %constant.69) | copy-start | bytes 1540
  79.0 59.0 %all-to-all-start = ((bf16[4,768,2,384]{1,3,2,0:T(8,128)(2,1)}), bf16[4,768,2,384]{1,3,2,0:T(8,128)(2,1)}, u32[]{:S(2)}, u32[]{:S(2)}) async-start(bf16[4,768,2,384]{1,3,2,0:T(8,128)(2,1)} %stack.23), calls=%async_computation | async-start | bytes 9437184 | tf_op jit(solution)/shard_map/all_to_all | solution.py:163
  162.6 46.0 %copy-start.8 = (bf16[1,48,3072]{2,1,0:T(8,128)(2,1)S(1)}, bf16[1,48,3072]{2,1,0:T(8,128)(2,1)}, u32[]{:S(2)}) copy-start(bf16[1,48,3072]{2,1,0:T(8,128)(2,1)} %param.19) | copy-start | bytes 884740
  167.9 85.9 %copy-start.3 = (f32[3,2,384,128]{2,3,0,1:T(8,128)}, f32[3,2,384,128]{2,3,0,1:T(8,128)S(1)}, u32[]{:S(2)}) copy-start(f32[3,2,384,128]{2,3,0,1:T(8,128)S(1)} %fusion.5) | copy-start | bytes 3538948
  217.8 35.0 %all-to-all-start.2 = ((bf16[48,8,256]{2,0,1:T(8,128)(2,1)}), bf16[48,8,256]{2,0,1:T(8,128)(2,1)}, u32[]{:S(2)}, u32[]{:S(2)}) async-start(bf16[48,8,256]{2,0,1:T(8,128)(2,1)} %bitcast.145), calls=%async_computation.2 | async-start | bytes 393216 | tf_op jit(solution)/shard_map/all_to_all | solution.py:177
  223.3 127.0 %reduce-scatter.2.cloned.1.call-start = ((), (), s32[]{:S(2)}) async-start(), calls=%async_computation.8 | async-start | bytes 2654208 | tf_op jit(solution)/shard_map/reduce_scatter | solution.py:180
  224.6 5.9 %copy-start.15 = (f32[128]{0:T(128)S(1)}, f32[128]{0:T(128)}, u32[]{:S(2)}) copy-start(f32[128]{0:T(128)} %constant.63.clone) | copy-start | bytes 1540
  232.3 23.0 %copy-start.11 = (bf16[2,384,128]{1,2,0:T(8,128)(2,1)}, bf16[2,384,128]{1,2,0:T(8,128)(2,1)S(1)}, u32[]{:S(2)}) copy-start(bf16[2,384,128]{1,2,0:T(8,128)(2,1)S(1)} %get-tuple-element.14) | copy-start | bytes 589828
  252.8 2.5 copy-start.13
  257.1 1.3 copy-start.4
  258.6 0.9 copy-start.12
  258.6 1.0 copy-start.14
  269.4 1.4 copy-start.6
  269.4 1.4 copy-start.7
  270.8 0.9 copy-start.10
  298.1 53.4 %copy-start.9 = (bf16[1,48,3072]{2,1,0:T(8,128)(2,1)S(1)}, bf16[1,48,3072]{2,1,0:T(8,128)(2,1)}, u32[]{:S(2)}) copy-start(bf16[1,48,3072]{2,1,0:T(8,128)(2,1)} %param.19) | copy-start | bytes 884740
  298.1 55.4 %copy-start.1 = (bf16[768,1152]{1,0:T(8,128)(2,1)S(1)}, bf16[768,1152]{1,0:T(8,128)(2,1)}, u32[]{:S(2)}) copy-start(bf16[768,1152]{1,0:T(8,128)(2,1)} %param.16) | copy-start | bytes 5308420
Sparse Core Ops, SparseCore 0:
  10.2 63.0 all-gather.6
  76.0 50.3 all-gather.4
  128.0 80.5 all-gather.8
  210.0 37.4 all-gather.10
  277.9 72.3 reduce-scatter.1
